TPU v7x, 32 devices: a whole 2x2x4 slice. The times are simulated.
32 devices in a mesh: tp: 2 (over x), sp: 16 (over z, y, core).
Axes of the slice: x: 2, y: 2, z: 4, core: 2. Of those that a mesh axis runs over, the one named last changes fastest.
Arguments:
- tokens: bfloat16 [2048, 2048], P('sp'), may hold values from -6 to 6
- item_lengths: int32 [4], replicated, may hold values from 128 to 1536, as said below
- first_gain: bfloat16 [2048], replicated, may hold values from 0.25 to 1.75
- query_weight: bfloat16 [2048, 2048], P('tp'), may hold values from -0.125 to 0.125
- key_weight: bfloat16 [1024, 2048], P('tp'), may hold values from -0.125 to 0.125
- value_weight: bfloat16 [1024, 2048], P('tp'), may hold values from -0.125 to 0.125
- headgate_weight: bfloat16 [16, 2048], P('tp'), may hold values from -0.125 to 0.125
- merge_weight: bfloat16 [2048, 2048], P(None, 'tp'), may hold values from -1 to 1
- query_norm: bfloat16 [128], replicated, may hold values from 0.8984375 to 2
- key_norm: bfloat16 [128], replicated, may hold values from 0.8984375 to 2
- second_gain: bfloat16 [2048], replicated, may hold values from 0.25 to 1.75
- gate_weight: bfloat16 [6144, 2048], P(('tp', 'sp')), may hold values from -0.125 to 0.125
- up_weight: bfloat16 [6144, 2048], P(('tp', 'sp')), may hold values from -0.125 to 0.125
- down_weight: bfloat16 [6144, 2048], P(('tp', 'sp')), may hold values from -0.078125 to 0.078125
- out_cotangent: bfloat16 [2048, 2048], P('sp')
Outputs:
- layer_output: bfloat16 [2048, 2048], P('sp')
- input_grad: float32 [2048, 2048], P('sp')
- first_grad: float32 [2048], replicated
- query_grad: float32 [2048, 2048], P('tp')
- key_grad: float32 [1024, 2048], P('tp')
- value_grad: float32 [1024, 2048], P('tp')
- headgate_grad: float32 [16, 2048], P('tp')
- merge_grad: float32 [2048, 2048], P(None, 'tp')
- query_norm_grad: float32 [128], replicated
- key_norm_grad: float32 [128], replicated
- second_grad: float32 [2048], replicated
- gate_grad: float32 [6144, 2048], P(('tp', 'sp'))
- up_grad: float32 [6144, 2048], P(('tp', 'sp'))
- down_grad: float32 [6144, 2048], P(('tp', 'sp'))
Inputs may be any that keep to these rules, and one draw needn't show every extreme that they name: `item_lengths`: the item lengths sum to 2048; exactly one item has 1536 tokens, every other at least 128.
All inputs are finite; a program needn't handle non-finite values.
Results may differ from a plain program's by a relative error of at most 0.02.
Values may be sent and summed in bfloat16 or wider, within the bound.
No kernel may reach another device: no remote copies, remote signals or barrier semaphores. Data moves between devices by JAX's collectives and lax.ppermute only.
A program may use at most 384 MiB of HBM per device.

v0:
```python
import math
import jax
import jax.numpy as jnp
from jax import lax
from jax.sharding import PartitionSpec as P

EPS = 1e-06
THETA = 1000000.0
NEG = -1e30


def right_dot(first_matrix, second_matrix):
    return lax.dot_general(
        first_matrix, second_matrix, (((1,), (1,)), ((), ())), preferred_element_type=jnp.float32
    )


def plain_dot(first_matrix, second_matrix):
    return jnp.dot(first_matrix, second_matrix, preferred_element_type=jnp.float32)


def outer_dot(first_matrix, second_matrix):
    return lax.dot_general(
        first_matrix, second_matrix, (((0,), (0,)), ((), ())), preferred_element_type=jnp.float32
    )


def normalize(values, gain_vector):
    inverse = lax.rsqrt(jnp.mean(values * values, axis=-1, keepdims=True) + EPS)
    return (values * inverse * gain_vector, inverse)


def normalize_back(values, inverse, gain_vector, upstream):
    weighted = upstream * gain_vector
    inner_mean = jnp.mean(weighted * values, axis=-1, keepdims=True)
    return (
        inverse * weighted - values * inverse * inverse * inverse * inner_mean,
        values * inverse * upstream,
    )


def rotary_tables(positions, head_width):
    half_width = head_width // 2
    frequency = THETA ** (-2.0 * jnp.arange(half_width, dtype=jnp.float32) / head_width)
    angles = positions.astype(jnp.float32)[:, None] * frequency[None, :]
    return (jnp.cos(angles)[:, None, :], jnp.sin(angles)[:, None, :])


def rotate(values, cosine_table, sine_table):
    half_width = values.shape[-1] // 2
    former = values[..., :half_width]
    latter = values[..., half_width:]
    return jnp.concatenate(
        [former * cosine_table - latter * sine_table, latter * cosine_table + former * sine_table],
        axis=-1,
    )


def item_geometry(item_lengths, first_row, row_count):
    item_ends = jnp.cumsum(item_lengths)
    item_starts = item_ends - item_lengths
    row_index = first_row + jnp.arange(row_count, dtype=jnp.int32)
    begins = jnp.max(
        jnp.where(item_starts[None, :] <= row_index[:, None], item_starts[None, :], 0), axis=1
    )
    return (row_index, begins)


def block_scores(queries, key_block, block_start, row_index, begins, score_scale):
    scores = (
        jnp.einsum("rkgd,skd->kgrs", queries, key_block, preferred_element_type=jnp.float32)
        * score_scale
    )
    key_index = block_start + jnp.arange(key_block.shape[0], dtype=jnp.int32)
    valid = (key_index[None, :] >= begins[:, None]) & (key_index[None, :] <= row_index[:, None])
    return (jnp.where(valid, scores, NEG), valid)


def swiglu(inputs_low, gate_rows, up_rows):
    gate_pre = right_dot(inputs_low, gate_rows)
    up_pre = right_dot(inputs_low, up_rows)
    return (gate_pre, up_pre, (jax.nn.silu(gate_pre) * up_pre).astype(jnp.bfloat16))


def swiglu_back(gate_pre, up_pre, grad_act):
    sigma = jax.nn.sigmoid(gate_pre)
    grad_gate = grad_act * up_pre * sigma * (1.0 + gate_pre * (1.0 - sigma))
    grad_up = grad_act * gate_pre * sigma
    return (grad_gate.astype(jnp.bfloat16), grad_up.astype(jnp.bfloat16))


def shards(
    tokens,
    item_lengths,
    first_gain,
    query_weight,
    key_weight,
    value_weight,
    headgate_weight,
    merge_weight,
    query_norm,
    key_norm,
    second_gain,
    gate_weight,
    up_weight,
    down_weight,
    out_cotangent,
):
    sp_size = lax.axis_size("sp")
    local_rows = tokens.shape[0]
    total_rows = local_rows * sp_size
    head_width = query_norm.shape[0]
    local_heads = query_weight.shape[0] // head_width
    local_groups = key_weight.shape[0] // head_width
    group_size = local_heads // local_groups
    score_scale = 1.0 / math.sqrt(head_width)
    first_row = lax.axis_index("sp") * local_rows
    row_index, begins = item_geometry(item_lengths, first_row, local_rows)
    cosine_table, sine_table = rotary_tables(row_index - begins, head_width)
    last_row = first_row + local_rows - 1
    first_begin = begins[0]
    residual = tokens.astype(jnp.float32)
    first_gain_f = first_gain.astype(jnp.float32)
    second_gain_f = second_gain.astype(jnp.float32)
    query_gain = query_norm.astype(jnp.float32)
    key_gain = key_norm.astype(jnp.float32)
    normed, first_inverse = normalize(residual, first_gain_f)
    normed_low = normed.astype(jnp.bfloat16)
    query_heads = right_dot(normed_low, query_weight).reshape(local_rows, local_heads, head_width)
    key_heads = right_dot(normed_low, key_weight).reshape(local_rows, local_groups, head_width)
    value_low = right_dot(normed_low, value_weight).astype(jnp.bfloat16)
    gate_logit = right_dot(normed_low, headgate_weight)
    query_unit, query_inverse = normalize(query_heads, query_gain)
    key_unit, key_inverse = normalize(key_heads, key_gain)
    queries = (
        rotate(query_unit, cosine_table, sine_table)
        .astype(jnp.bfloat16)
        .reshape(local_rows, local_groups, group_size, head_width)
    )
    keys_low = (
        rotate(key_unit, cosine_table, sine_table)
        .astype(jnp.bfloat16)
        .reshape(local_rows, local_groups * head_width)
    )
    keys_all, values_all = (
        lax.all_gather(keys_low, "sp", axis=0, tiled=True),
        lax.all_gather(value_low, "sp", axis=0, tiled=True),
    )
    block_size = math.gcd(total_rows, 1024)
    block_count = total_rows // block_size
    key_blocks = keys_all.reshape(block_count, block_size, local_groups, head_width)
    value_blocks = values_all.reshape(block_count, block_size, local_groups, head_width)
    block_starts = jnp.arange(block_count, dtype=jnp.int32) * block_size

    def needed(block_start):
        return (block_start <= last_row) & (block_start + block_size > first_begin)

    def first_pass(carried, inputs):
        key_block, value_block, block_start = inputs

        def first_update(current):
            running_max, running_sum = current
            scores, valid = block_scores(
                queries, key_block, block_start, row_index, begins, score_scale
            )
            new_max = jnp.maximum(running_max, jnp.max(scores, axis=-1))
            weights = jnp.where(valid, jnp.exp(scores - new_max[..., None]), 0.0)
            return (
                new_max,
                running_sum * jnp.exp(running_max - new_max) + jnp.sum(weights, axis=-1),
            )

        def first_unchanged(current):
            return current

        return (lax.cond(needed(block_start), first_update, first_unchanged, carried), None)

    start_max = jnp.full((local_groups, group_size, local_rows), NEG, jnp.float32)
    start_sum = jnp.zeros((local_groups, group_size, local_rows), jnp.float32)
    (running_max, running_sum), _ = lax.scan(
        first_pass, (start_max, start_sum), (key_blocks, value_blocks, block_starts)
    )
    log_total = running_max + jnp.log(running_sum)

    def second_pass(carried, inputs):
        key_block, value_block, block_start = inputs

        def second_update(current):
            scores, valid = block_scores(
                queries, key_block, block_start, row_index, begins, score_scale
            )
            probs = jnp.where(valid, jnp.exp(scores - log_total[..., None]), 0.0).astype(
                jnp.bfloat16
            )
            return current + jnp.einsum(
                "kgrs,skd->kgrd", probs, value_block, preferred_element_type=jnp.float32
            )

        def second_unchanged(current):
            return current

        return (lax.cond(needed(block_start), second_update, second_unchanged, carried), None)

    start_acc = jnp.zeros((local_groups, group_size, local_rows, head_width), jnp.float32)
    accumulated, _ = lax.scan(second_pass, start_acc, (key_blocks, value_blocks, block_starts))
    attended = jnp.transpose(accumulated, (2, 0, 1, 3)).reshape(local_rows, local_heads, head_width)
    gate_value = jax.nn.sigmoid(gate_logit)
    gated_low = (
        (attended * gate_value[..., None])
        .astype(jnp.bfloat16)
        .reshape(local_rows, local_heads * head_width)
    )
    attention_out = lax.psum(right_dot(gated_low, merge_weight).astype(jnp.bfloat16), "tp").astype(
        jnp.float32
    )
    hidden = residual + attention_out
    normed_second, second_inverse = normalize(hidden, second_gain_f)
    second_low = normed_second.astype(jnp.bfloat16)
    acts_all = swiglu(lax.all_gather(second_low, "sp", axis=0, tiled=True), gate_weight, up_weight)[
        2
    ]
    branch_part = lax.psum_scatter(
        plain_dot(acts_all, down_weight), "sp", scatter_dimension=0, tiled=True
    )
    branch_out = lax.psum(branch_part.astype(jnp.bfloat16), "tp").astype(jnp.float32)
    layer_output = (hidden + branch_out).astype(jnp.bfloat16)
    grad_out = out_cotangent.astype(jnp.float32)
    stacked_weights = jnp.concatenate([gate_weight, up_weight], axis=0)
    inputs_low = lax.all_gather(second_low, "sp", axis=0, tiled=True)
    grads_low = lax.all_gather(out_cotangent, "sp", axis=0, tiled=True)
    gate_pre, up_pre, act_low = swiglu(inputs_low, gate_weight, up_weight)
    grad_act = right_dot(grads_low, down_weight)
    grad_gate, grad_up = swiglu_back(gate_pre, up_pre, grad_act)
    gate_acc = outer_dot(grad_gate, inputs_low)
    up_acc = outer_dot(grad_up, inputs_low)
    down_acc = outer_dot(act_low, grads_low)
    fold_stacked_grads = jnp.concatenate([grad_gate, grad_up], axis=1)
    second_part = lax.psum_scatter(
        plain_dot(fold_stacked_grads, stacked_weights), "sp", scatter_dimension=0, tiled=True
    )
    grad_second = lax.psum(second_part.astype(jnp.bfloat16), "tp").astype(jnp.float32)
    grad_hidden_norm, second_terms = normalize_back(
        hidden, second_inverse, second_gain_f, grad_second
    )
    hidden_grad = grad_out + grad_hidden_norm
    hidden_low = hidden_grad.astype(jnp.bfloat16)
    merge_grad = outer_dot(hidden_low, gated_low)
    grad_gated = plain_dot(hidden_low, merge_weight).reshape(local_rows, local_heads, head_width)
    grad_attended_low = (grad_gated * gate_value[..., None]).astype(jnp.bfloat16)
    grad_logit_low = (
        jnp.sum(grad_gated * attended, axis=-1) * gate_value * (1.0 - gate_value)
    ).astype(jnp.bfloat16)
    row_delta = jnp.sum(grad_attended_low.astype(jnp.float32) * attended, axis=-1).reshape(
        local_rows, local_groups, group_size
    )
    row_delta = jnp.transpose(row_delta, (1, 2, 0))
    grad_grouped = grad_attended_low.reshape(local_rows, local_groups, group_size, head_width)

    def back_pass(carried, inputs):
        key_block, value_block, block_start = inputs

        def back_update(grad_queries):
            scores, valid = block_scores(
                queries, key_block, block_start, row_index, begins, score_scale
            )
            probs = jnp.where(valid, jnp.exp(scores - log_total[..., None]), 0.0)
            grad_probs = jnp.einsum(
                "rkgd,skd->kgrs", grad_grouped, value_block, preferred_element_type=jnp.float32
            )
            grad_scores = (probs * (grad_probs - row_delta[..., None])).astype(jnp.bfloat16)
            grad_queries = (
                grad_queries
                + jnp.einsum(
                    "kgrs,skd->rkgd", grad_scores, key_block, preferred_element_type=jnp.float32
                )
                * score_scale
            )
            grad_keys = (
                jnp.einsum(
                    "kgrs,rkgd->skd", grad_scores, queries, preferred_element_type=jnp.float32
                )
                * score_scale
            )
            grad_values = jnp.einsum(
                "kgrs,rkgd->skd",
                probs.astype(jnp.bfloat16),
                grad_grouped,
                preferred_element_type=jnp.float32,
            )
            return (grad_queries, (grad_keys, grad_values))

        def skipped(grad_queries):
            empty = jnp.zeros((block_size, local_groups, head_width), jnp.float32)
            return (grad_queries, (empty, empty))

        return lax.cond(needed(block_start), back_update, skipped, carried)

    start_queries = jnp.zeros((local_rows, local_groups, group_size, head_width), jnp.float32)
    grad_queries, (key_parts, value_parts) = lax.scan(
        back_pass, start_queries, (key_blocks, value_blocks, block_starts)
    )
    key_terms = key_parts.reshape(total_rows, local_groups * head_width)
    value_terms = value_parts.reshape(total_rows, local_groups * head_width)
    key_sum, value_sum = (
        lax.psum_scatter(key_terms, "sp", scatter_dimension=0, tiled=True),
        lax.psum_scatter(value_terms, "sp", scatter_dimension=0, tiled=True),
    )
    grad_query_unit = rotate(
        grad_queries.reshape(local_rows, local_heads, head_width), cosine_table, -sine_table
    )
    grad_query_raw, query_gain_terms = normalize_back(
        query_heads, query_inverse, query_gain, grad_query_unit
    )
    grad_key_unit = rotate(
        key_sum.reshape(local_rows, local_groups, head_width), cosine_table, -sine_table
    )
    grad_key_raw, key_gain_terms = normalize_back(key_heads, key_inverse, key_gain, grad_key_unit)
    query_low = grad_query_raw.reshape(local_rows, local_heads * head_width).astype(jnp.bfloat16)
    key_low = grad_key_raw.reshape(local_rows, local_groups * head_width).astype(jnp.bfloat16)
    value_grad_low = value_sum.astype(jnp.bfloat16)
    query_grad = outer_dot(query_low, normed_low)
    key_grad = outer_dot(key_low, normed_low)
    value_grad = outer_dot(value_grad_low, normed_low)
    headgate_grad = outer_dot(grad_logit_low, normed_low)
    input_part = (
        plain_dot(query_low, query_weight)
        + plain_dot(key_low, key_weight)
        + plain_dot(value_grad_low, value_weight)
        + plain_dot(grad_logit_low, headgate_weight)
    )
    input_sum, query_gain_sum, key_gain_sum = (
        lax.psum(input_part.astype(jnp.bfloat16), "tp").astype(jnp.float32),
        lax.psum(jnp.sum(query_gain_terms, axis=(0, 1)).astype(jnp.bfloat16), "tp").astype(
            jnp.float32
        ),
        lax.psum(jnp.sum(key_gain_terms, axis=(0, 1)).astype(jnp.bfloat16), "tp").astype(
            jnp.float32
        ),
    )
    grad_residual_norm, first_terms = normalize_back(
        residual, first_inverse, first_gain_f, input_sum
    )
    input_grad = hidden_grad + grad_residual_norm
    reduced = lax.psum(
        (
            query_grad,
            key_grad,
            value_grad,
            headgate_grad,
            merge_grad,
            query_gain_sum,
            key_gain_sum,
            jnp.sum(first_terms, axis=0),
            jnp.sum(second_terms, axis=0),
        ),
        "sp",
    )
    return (
        layer_output,
        input_grad,
        reduced[7],
        reduced[0],
        reduced[1],
        reduced[2],
        reduced[3],
        reduced[4],
        reduced[5],
        reduced[6],
        reduced[8],
        gate_acc,
        up_acc,
        down_acc,
    )


def solution(mesh):
    return jax.shard_map(
        shards,
        mesh=mesh,
        in_specs=(
            P("sp", None),
            P(),
            P(),
            P("tp", None),
            P("tp", None),
            P("tp", None),
            P("tp", None),
            P(None, "tp"),
            P(),
            P(),
            P(),
            P(("tp", "sp"), None),
            P(("tp", "sp"), None),
            P(("tp", "sp"), None),
            P("sp", None),
        ),
        out_specs=(
            P("sp", None),
            P("sp", None),
            P(),
            P("tp", None),
            P("tp", None),
            P("tp", None),
            P("tp", None),
            P(None, "tp"),
            P(),
            P(),
            P(),
            P(("tp", "sp"), None),
            P(("tp", "sp"), None),
            P(("tp", "sp"), None),
        ),
        check_vma=False,
    )
```

profile of v0, /device:TPU:0, one launch (start us, length us, event | category | flops | bytes accessed | tf_op | source)
XLA Modules:
  0.0 1403.6 jit_solution(12109485041984418641)
XLA Ops:
  24.9 32.0 %all-gather.7.cloned.1.call-done = bf16[2048,512]{1,0:T(8,128)(2,1)} async-done(((bf16[128,512]{1,0:T(8,128)(2,1)}), bf16[2048,512]{1,0:T(8,128)(2,1)}) %all-gather.7.cloned.1.call-update) | async-done | bytes 2097168 | tf_op jit(solution)/shard_map/all_gather | solution.py:147
  64.0 35.8 %all-gather.5.cloned.1.call-done = bf16[2048,512]{1,0:T(8,128)(2,1)} async-done(((bf16[128,512]{1,0:T(8,128)(2,1)}), bf16[2048,512]{1,0:T(8,128)(2,1)}) %all-gather.5.cloned.1.call-update) | async-done | bytes 2097168 | tf_op jit(solution)/shard_map/all_gather | solution.py:146
  106.9 7.9 while.45
  114.9 8.3 while.46
  126.1 4.5 convolution_convert_fusion
  131.5 35.0 %all-reduce.9.cloned.1.call-done = bf16[128,2048]{1,0:T(8,128)(2,1)} async-done(((bf16[128,2048]{1,0:T(8,128)(2,1)}), bf16[128,2048]{1,0:T(8,128)(2,1)}) %all-reduce.9.cloned.1.call-update) | async-done | bytes 524304 | tf_op jit(solution)/shard_map/psum | solution.py:213
  170.0 73.8 %all-gather.11.cloned.1.call-done = bf16[2048,2048]{1,0:T(8,128)(2,1)} async-done(((bf16[128,2048]{1,0:T(8,128)(2,1)}), bf16[2048,2048]{1,0:T(8,128)(2,1)}) %all-gather.11.cloned.1.call-update) | async-done | bytes 8388624 | tf_op jit(solution)/shard_map/all_gather | solution.py:230
  243.7 7.6 fusion.129
  251.3 68.4 %all-gather.9.cloned.1.call-done = bf16[2048,2048]{1,0:T(8,128)(2,1)} async-done(((bf16[128,2048]{1,0:T(8,128)(2,1)}), bf16[2048,2048]{1,0:T(8,128)(2,1)}) %all-gather.9.cloned.1.call-update) | async-done | bytes 8388624 | tf_op jit(solution)/shard_map/all_gather | solution.py:219
  319.7 6.6 fusion.127
  331.8 8.2 fusion.61
  340.1 176.9 %reduce-scatter.7.cloned.1.call-done = f32[128,2048]{1,0:T(8,128)} async-done(((f32[2048,2048]{1,0:T(8,128)}), f32[128,2048]{1,0:T(8,128)}) %reduce-scatter.7.cloned.1.call-update) | async-done | bytes 1048592 | tf_op jit(solution)/shard_map/reduce_scatter | solution.py:238
  519.2 9.6 fusion.128
  529.1 18.5 %all-reduce.11.cloned.1.call-done = bf16[128,2048]{1,0:T(8,128)(2,1)} async-done(((bf16[128,2048]{1,0:T(8,128)(2,1)}), bf16[128,2048]{1,0:T(8,128)(2,1)}) %all-reduce.11.cloned.1.call-update) | async-done | bytes 524304 | tf_op jit(solution)/shard_map/psum | solution.py:241
  559.1 31.8 %while.47 = (s32[]{:T(128)}, f32[128,4,2,128]{3,0,2,1:T(8,128)S(1)}, f32[2,1024,4,128]{3,2,1,0:T(4,128)}, f32[2,1024,4,128]{3,2,1,0:T(4,128)}, s32[2]{0:T(128)S(...) while((s32[]{:T(128)}, ...), condition=%wide.region_26.27_spmd.clone, body=%wide.region_23.26_spmd.clone.sunk | while | flops 1355940992 | bytes 54943664 | solution.py:299
  561.0 10.3 conditional.11
  571.4 7.7 copy_dynamic-update-slice_fusion.3
  584.0 6.9 copy_dynamic-update-slice_fusion.3
  590.9 4.6 copy.160
  595.6 4.7 copy.159
  602.2 128.2 %reduce-scatter.5.cloned.1.call-done = f32[128,2048]{1,0:T(8,128)} async-done(((f32[2048,2048]{1,0:T(8,128)}), f32[128,2048]{1,0:T(8,128)}) %reduce-scatter.5.cloned.1.call-update) | async-done | bytes 1048592 | tf_op jit(solution)/shard_map/reduce_scatter | solution.py:222
  741.5 4.9 fusion.102
  746.4 59.9 %reduce-scatter.9.cloned.1.call-done = f32[128,512]{1,0:T(8,128)} async-done(((f32[2048,512]{1,0:T(8,128)}), f32[128,512]{1,0:T(8,128)}) %reduce-scatter.9.cloned.1.call-update) | async-done | bytes 262160 | tf_op jit(solution)/shard_map/reduce_scatter | solution.py:305
  814.7 67.7 %reduce-scatter.11.cloned.1.call-done = f32[128,512]{1,0:T(8,128)} async-done(((f32[2048,512]{1,0:T(8,128)}), f32[128,512]{1,0:T(8,128)}) %reduce-scatter.11.cloned.1.call-update) | async-done | bytes 262160 | tf_op jit(solution)/shard_map/reduce_scatter | solution.py:306
  886.2 5.5 fusion.118
  897.4 6.8 fusion.133
  904.2 6.5 fusion.131
  913.8 5.0 all-reduce.2
  918.8 6.7 all-reduce.15.cloned.1.call-done
  927.2 64.4 %all-reduce = (f32[2048]{0:T(1024)}, f32[128]{0:T(128)}, f32[128]{0:T(128)}, f32[2048]{0:T(1024)}) all-reduce(f32[2048]{0:T(1024)S(1)} %get-tuple-element.661, bf16[128]{0:T(256)(128)(2,1)S(1)} %get-tuple-element.744, bf16[128]{0:T(256)(128)(2,1)S(1)} %get-tuple-element.745, ...), channel_id=1, replica_groups=mesh['tp'=2,'sp'=16] {'sp'}, use_global_device_ids=true, to_apply=%region_35.36 | all-reduce | flops 4352 | bytes 34304 | tf_op jit(solution)/shard_map/psum | solution.py:344
  995.2 382.0 %all-reduce.13.cloned.1.call-done = (f32[1024,2048]{1,0:T(8,128)}, f32[512,2048]{1,0:T(8,128)}, f32[512,2048]{1,0:T(8,128)}, f32[8,2048]{1,0:T(8,128)}, f32[2048,1024]{1,0:T(8,128)}) async-done(((f32[1024,2048]{1,0:T(8,128)}, f32[512,2048]{1,0:T(8,128)}, f32[512,2048]{1,0:T(8,128)}, f32[8,2048]{1,0:T(8,128)}, f32[2048,1024]{1,0:T(8,128)}), (f32[1024,2048]{1,0:T(8,128)}, f32[512,2048]{1,0:T(8,128)}, ...) | async-done | bytes 25231376 | tf_op jit(solution)/shard_map/psum | solution.py:344
  1377.2 8.0 copy.216
  (318 shorter events, 144.7 us)
Async XLA Ops:
  7.2 49.6 %all-gather.7.cloned.1.call-start = ((), (), s32[]{:S(2)}) async-start(), calls=%async_computation.5 | async-start | bytes 2228224 | tf_op jit(solution)/shard_map/all_gather | solution.py:147
  8.6 15.9 %copy-start.47 = (f32[128]{0:T(128)}, f32[128]{0:T(128)S(1)}, u32[]{:S(2)}) copy-start(f32[128]{0:T(128)S(1)} %add_rsqrt_fusion.3) | copy-start | bytes 1540
  9.3 15.2 %copy-start.38 = (f32[2048]{0:T(1024)}, f32[2048]{0:T(1024)S(1)}, u32[]{:S(2)}) copy-start(f32[2048]{0:T(1024)S(1)} %convert_element_type.143) | copy-start | bytes 24580
  9.3 9.0 copy-start.71
  9.3 9.0 copy-start.1
  12.7 87.1 %all-gather.5.cloned.1.call-start = ((), (), s32[]{:S(2)}) async-start(), calls=%async_computation.4 | async-start | bytes 2228224 | tf_op jit(solution)/shard_map/all_gather | solution.py:146
  18.3 148.3 %all-reduce.9.cloned.1.call-start = ((), (), s32[]{:S(2)}) async-start(), calls=%async_computation.6 | async-start | bytes 1048576 | tf_op jit(solution)/shard_map/psum | solution.py:213
  24.9 530.5 %copy-start.42 = (f32[128,8]{0,1:T(8,128)}, f32[128,8]{0,1:T(8,128)S(1)}, u32[]{:S(2)}) copy-start(f32[128,8]{0,1:T(8,128)S(1)} %fusion.76) | copy-start | bytes 12292
  125.3 44.6 %copy-start.10 = (f32[4,2,128,128]{2,3,1,0:T(8,128)}, f32[4,2,128,128]{2,3,1,0:T(8,128)S(1)}, u32[]{:S(2)}) copy-start(f32[4,2,128,128]{2,3,1,0:T(8,128)S(1)} %copy.82) | copy-start | bytes 1572868
  130.7 113.1 %all-gather.11.cloned.1.call-start = ((), (), s32[]{:S(2)}) async-start(), calls=%async_computation.9 | async-start | bytes 8912896 | tf_op jit(solution)/shard_map/all_gather | solution.py:230
  131.3 188.4 %all-gather.9.cloned.1.call-start = ((), (), s32[]{:S(2)}) async-start(), calls=%async_computation.7 | async-start | bytes 8912896 | tf_op jit(solution)/shard_map/all_gather | solution.py:219
  167.8 381.9 %copy-start.53 = (f32[128]{0:T(128)}, f32[128]{0:T(128)S(1)}, u32[]{:S(2)}) copy-start(f32[128]{0:T(128)S(1)} %add_rsqrt_fusion.2) | copy-start | bytes 1540
  169.9 347.1 %reduce-scatter.7.cloned.1.call-start = ((), (), s32[]{:S(2)}) async-start(), calls=%async_computation.10 | async-start | bytes 17825792 | tf_op jit(solution)/shard_map/reduce_scatter | solution.py:238
  340.1 207.6 %all-reduce.11.cloned.1.call-start = ((), (), s32[]{:S(2)}) async-start(), calls=%async_computation.11 | async-start | bytes 1048576 | tf_op jit(solution)/shard_map/psum | solution.py:241
  519.2 211.2 %reduce-scatter.5.cloned.1.call-start = ((), (), s32[]{:S(2)}) async-start(), calls=%async_computation.8 | async-start | bytes 17825792 | tf_op jit(solution)/shard_map/reduce_scatter | solution.py:222
  528.8 18.9 %copy-start.4 = (bf16[128,2048]{1,0:T(8,128)(2,1)S(1)}, bf16[128,2048]{1,0:T(8,128)(2,1)}, u32[]{:S(2)}) copy-start(bf16[128,2048]{1,0:T(8,128)(2,1)} %all-reduce.9.cloned.1.call-done) | copy-start | bytes 1572868
  528.8 277.5 %reduce-scatter.9.cloned.1.call-start = ((), (), s32[]{:S(2)}) async-start(), calls=%async_computation.12 | async-start | bytes 4456448 | tf_op jit(solution)/shard_map/reduce_scatter | solution.py:305
  549.8 9.3 copy-start.68
  549.8 9.3 copy-start.73
  595.6 286.9 %reduce-scatter.11.cloned.1.call-start = ((), (), s32[]{:S(2)}) async-start(), calls=%async_computation.13 | async-start | bytes 4456448 | tf_op jit(solution)/shard_map/reduce_scatter | solution.py:306
  600.3 134.8 %copy-start.43 = (f32[128,8]{0,1:T(8,128)S(1)}, f32[128,8]{0,1:T(8,128)}, u32[]{:S(2)}) copy-start(f32[128,8]{0,1:T(8,128)} %copy-done.42) | copy-start | bytes 12292
  600.3 135.1 %copy-start.26 = (f32[128,64]{1,0:T(8,128)S(1)}, f32[128,64]{1,0:T(8,128)}, u32[]{:S(2)}) copy-start(f32[128,64]{1,0:T(8,128)} %copy-done.25) | copy-start | bytes 98308
  600.3 135.1 %copy-start.34 = (f32[128,64]{1,0:T(8,128)S(1)}, f32[128,64]{1,0:T(8,128)}, u32[]{:S(2)}) copy-start(f32[128,64]{1,0:T(8,128)} %get-tuple-element.777) | copy-start | bytes 98308
  600.3 325.2 %all-reduce.15.cloned.1.call-start = ((), (), s32[]{:S(2)}) async-start(), calls=%async_computation.15 | async-start | bytes 2097152 | tf_op jit(solution)/shard_map/psum | solution.py:225
  741.5 67.8 %copy-start.17 = (f32[128,4,128]{2,1,0:T(4,128)S(1)}, f32[128,4,128]{2,1,0:T(4,128)}, u32[]{:S(2)}) copy-start(f32[128,4,128]{2,1,0:T(4,128)} %copy-done.16) | copy-start | bytes 786436
  814.7 71.5 %copy-start.20 = (bf16[128,1024]{1,0:T(8,128)(2,1)S(1)}, bf16[128,1024]{1,0:T(8,128)(2,1)}, u32[]{:S(2)}) copy-start(bf16[128,1024]{1,0:T(8,128)(2,1)} %copy-done.19) | copy-start | bytes 786436
  886.0 491.2 %all-reduce.13.cloned.1.call-start = ((), (), s32[]{:S(2)}) async-start(), calls=%async_computation.14 | async-start | bytes 50462720 | tf_op jit(solution)/shard_map/psum | solution.py:344
  897.4 13.3 slice-start.2
  910.7 14.8 %copy-start.50 = (f32[128]{0:T(128)S(1)}, f32[128]{0:T(128)}, u32[]{:S(2)}) copy-start(f32[128]{0:T(128)} %copy-done.47) | copy-start | bytes 1540
  910.7 16.4 %copy-start.44 = (f32[2048]{0:T(1024)S(1)}, f32[2048]{0:T(1024)}, u32[]{:S(2)}) copy-start(f32[2048]{0:T(1024)} %get-tuple-element.659) | copy-start | bytes 24580
  910.7 80.8 %copy-start.55 = (f32[128]{0:T(128)S(1)}, f32[128]{0:T(128)}, u32[]{:S(2)}) copy-start(f32[128]{0:T(128)} %copy-done.53) | copy-start | bytes 1540
  910.8 80.8 %copy-start.61 = (f32[128]{0:T(128)S(1)}, f32[128]{0:T(128)}, u32[]{:S(2)}) copy-start(f32[128]{0:T(128)} %copy-done.59) | copy-start | bytes 1540
  (59 other events, 240.7 us)
Sparse Core Ops, SparseCore 0:
  12.8 44.0 all-gather.6
  59.6 40.1 all-gather.4
  130.8 35.7 all-reduce.8
  168.8 74.8 all-gather.10
  246.5 73.1 all-gather.8
  340.2 176.8 reduce-scatter.6
  520.0 27.5 all-reduce.10
  551.7 178.5 reduce-scatter.4
  734.8 71.4 reduce-scatter.8
  811.0 71.3 reduce-scatter.10
  886.1 39.4 all-reduce.14
  932.2 444.9 all-reduce.12
where the time goes:
time: 1410 us; the launch traced here: 1400 us
  waiting for transfers between devices  1090 us (77%)
  matrix products  109 us (8%)
  local copies, waits for them, and re-layouts  80.7 us (6%)
  blocking collectives  69.4 us (5%)
  other arithmetic  33.8 us (2%)
  between operations  15.4 us (1%)
    psum x1, waiting for transfers between devices, shards(): lax.psum((query_grad, key_grad, value_grad, headgate_grad, merge_grad, qu...  382 us
    reduce_scatter x1, waiting for transfers between devices, shards(): lax.psum_scatter(plain_dot(fold_stacked_grads, stacked_weights), 'sp', sc...  177 us
    reduce_scatter x1, waiting for transfers between devices, shards(): lax.psum_scatter(plain_dot(acts_all, down_weight), 'sp', scatter_dimensio...  128 us
    all_gather x1, waiting for transfers between devices, shards(): grads_low = lax.all_gather(out_cotangent, 'sp', axis=0, tiled=True)  73.8 us
    all_gather x1, waiting for transfers between devices, shards(): lax.all_gather(second_low, 'sp', axis=0, tiled=True)  68.4 us
    reduce_scatter x1, waiting for transfers between devices, shards(): lax.psum_scatter(value_terms, 'sp', scatter_dimension=0, tiled=True)  67.7 us
    psum x1, blocking collectives, shards(): lax.psum((query_grad, key_grad, value_grad, headgate_grad, merge_grad, qu...  64.4 us
    reduce_scatter x1, waiting for transfers between devices, shards(): lax.psum_scatter(key_terms, 'sp', scatter_dimension=0, tiled=True)  59.9 us
  transfers between devices with their start and end apart: 12, of which 12 were waited for; matrix products, arithmetic and copies ran while one was open for 10% of the time, Pallas kernels for 0%

commit v1 on v0

--- a/solution.py
+++ b/solution.py
@@ -226,8 +226,13 @@
     layer_output = (hidden + branch_out).astype(jnp.bfloat16)
     grad_out = out_cotangent.astype(jnp.float32)
     stacked_weights = jnp.concatenate([gate_weight, up_weight], axis=0)
-    inputs_low = lax.all_gather(second_low, "sp", axis=0, tiled=True)
-    grads_low = lax.all_gather(out_cotangent, "sp", axis=0, tiled=True)
+    inputs_low, grads_low = jnp.split(
+        lax.all_gather(
+            jnp.concatenate([second_low, out_cotangent], axis=1), "sp", axis=0, tiled=True
+        ),
+        [second_low.shape[1]],
+        axis=1,
+    )
     gate_pre, up_pre, act_low = swiglu(inputs_low, gate_weight, up_weight)
     grad_act = right_dot(grads_low, down_weight)
     grad_gate, grad_up = swiglu_back(gate_pre, up_pre, grad_act)

time: 1410 us -> 1450 us (1.028)
  waiting for transfers between devices: 1090 us -> 1110 us
  matrix products: 109 us -> 126 us
    all_gather x1, waiting for transfers between devices: 73.8 us -> 126 us  [shards(): lax.all_gather(jnp.concatenate([second_low, out_cotangent], axis=1), 'sp'...]
    all_gather x1, waiting for transfers between devices: 68.4 us -> 47.9 us  [shards(): lax.all_gather(second_low, 'sp', axis=0, tiled=True)]
    dot_general x8 -> x9, matrix products: 32.2 us -> 39.7 us  [right_dot(): lax.dot_general(first_matrix, second_matrix, (((1,), (1,)), ((), ())), pr...]
    unnamed x165 -> x173, local copies, waits for them, and re-layouts: 44.1 us -> 44.9 us
  transfers between devices with their start and end apart: 12 -> 12, of which waited for: 12 -> 12; matrix products, arithmetic and copies ran while one was open for 10% -> 12% of each run, Pallas kernels for 0% -> 0%
where the time goes in v1:
time: 1450 us; the launch traced here: 1440 us
  waiting for transfers between devices  1110 us (77%)
  matrix products  126 us (9%)
  local copies, waits for them, and re-layouts  81.5 us (6%)
  blocking collectives  69.3 us (5%)
  other arithmetic  35.8 us (2%)
  between operations  15.7 us (1%)
    psum x1, waiting for transfers between devices, shards(): lax.psum((query_grad, key_grad, value_grad, headgate_grad, merge_grad, qu...  382 us
    reduce_scatter x1, waiting for transfers between devices, shards(): lax.psum_scatter(plain_dot(fold_stacked_grads, stacked_weights), 'sp', sc...  174 us
    reduce_scatter x1, waiting for transfers between devices, shards(): lax.psum_scatter(plain_dot(acts_all, down_weight), 'sp', scatter_dimensio...  128 us
    all_gather x1, waiting for transfers between devices, shards(): lax.all_gather(jnp.concatenate([second_low, out_cotangent], axis=1), 'sp'...  126 us
    reduce_scatter x1, waiting for transfers between devices, shards(): lax.psum_scatter(value_terms, 'sp', scatter_dimension=0, tiled=True)  67.7 us
    psum x1, blocking collectives, shards(): lax.psum((query_grad, key_grad, value_grad, headgate_grad, merge_grad, qu...  64.4 us
    reduce_scatter x1, waiting for transfers between devices, shards(): lax.psum_scatter(key_terms, 'sp', scatter_dimension=0, tiled=True)  59.9 us
    all_gather x1, waiting for transfers between devices, shards(): lax.all_gather(second_low, 'sp', axis=0, tiled=True)  47.9 us
  transfers between devices with their start and end apart: 12, of which 12 were waited for; matrix products, arithmetic and copies ran while one was open for 12% of the time, Pallas kernels for 0%

profile of v1, /device:TPU:0, one launch (start us, length us, event | category | flops | bytes accessed | tf_op | source)
XLA Modules:
  0.0 1443.8 jit_solution(9714655518298584536)
XLA Ops:
  24.8 32.0 %all-gather.7.cloned.1.call-done = bf16[2048,512]{1,0:T(8,128)(2,1)} async-done(((bf16[128,512]{1,0:T(8,128)(2,1)}), bf16[2048,512]{1,0:T(8,128)(2,1)}) %all-gather.7.cloned.1.call-update) | async-done | bytes 2097168 | tf_op jit(solution)/shard_map/all_gather | solution.py:147
  64.0 35.8 %all-gather.5.cloned.1.call-done = bf16[2048,512]{1,0:T(8,128)(2,1)} async-done(((bf16[128,512]{1,0:T(8,128)(2,1)}), bf16[2048,512]{1,0:T(8,128)(2,1)}) %all-gather.5.cloned.1.call-update) | async-done | bytes 2097168 | tf_op jit(solution)/shard_map/all_gather | solution.py:146
  106.9 7.9 while.45
  114.8 8.3 while.46
  131.8 35.4 %all-reduce.9.cloned.1.call-done = bf16[128,2048]{1,0:T(8,128)(2,1)} async-done(((bf16[128,2048]{1,0:T(8,128)(2,1)}), bf16[128,2048]{1,0:T(8,128)(2,1)}) %all-reduce.9.cloned.1.call-update) | async-done | bytes 524304 | tf_op jit(solution)/shard_map/psum | solution.py:213
  173.4 126.4 %all-gather.11.cloned.1.call-done = bf16[2048,4096]{1,0:T(8,128)(2,1)} async-done(((bf16[128,4096]{1,0:T(8,128)(2,1)}), bf16[2048,4096]{1,0:T(8,128)(2,1)}) %all-gather.11.cloned.1.call-update) | async-done | bytes 16777232 | tf_op jit(solution)/shard_map/all_gather | solution.py:230
  299.8 6.6 fusion.70
  306.4 7.4 fusion.62
  319.4 8.2 fusion.75
  327.8 47.9 %all-gather.9.cloned.1.call-done = bf16[2048,2048]{1,0:T(8,128)(2,1)} async-done(((bf16[128,2048]{1,0:T(8,128)(2,1)}), bf16[2048,2048]{1,0:T(8,128)(2,1)}) %all-gather.9.cloned.1.call-update) | async-done | bytes 8388624 | tf_op jit(solution)/shard_map/all_gather | solution.py:219
  375.7 7.6 fusion.150
  383.3 173.8 %reduce-scatter.7.cloned.1.call-done = f32[128,2048]{1,0:T(8,128)} async-done(((f32[2048,2048]{1,0:T(8,128)}), f32[128,2048]{1,0:T(8,128)}) %reduce-scatter.7.cloned.1.call-update) | async-done | bytes 1048592 | tf_op jit(solution)/shard_map/reduce_scatter | solution.py:243
  559.2 15.2 %fusion.74 = f32[2048,2048]{1,0:T(8,128)} fusion(bf16[192,2048]{1,0:T(8,128)(2,1)} %param.40, bf16[2048,2048]{1,0:T(8,128)(2,1)} %all-gather.9.cloned.1.call-done, bf16[192,2048]{1,0:T(8,128)(2,1)} %param.39, f32[2048,192]{0,1:T(8,128)} %fusion.150), kind=kOutput, calls=%fused_computation.91 | convolution fusion | flops 3223584768 | bytes 28311552 | tf_op jit(solution)/shard_map/dot_general | solution.py:19
  574.7 12.9 all-reduce.11.cloned.1.call-done
  599.1 31.8 %while.47 = (s32[]{:T(128)}, f32[128,4,2,128]{3,0,2,1:T(8,128)S(1)}, f32[2,1024,4,128]{3,2,1,0:T(4,128)}, f32[2,1024,4,128]{3,2,1,0:T(4,128)}, s32[2]{0:T(128)S(...) while((s32[]{:T(128)}, ...), condition=%wide.region_26.27_spmd.clone, body=%wide.region_23.26_spmd.clone.sunk | while | flops 1355940992 | bytes 54943664 | solution.py:304
  601.0 10.3 conditional.11
  611.3 7.7 copy_dynamic-update-slice_fusion.3
  623.9 6.9 copy_dynamic-update-slice_fusion.3
  630.8 4.6 copy.160
  635.6 4.7 copy.159
  642.1 128.3 %reduce-scatter.5.cloned.1.call-done = f32[128,2048]{1,0:T(8,128)} async-done(((f32[2048,2048]{1,0:T(8,128)}), f32[128,2048]{1,0:T(8,128)}) %reduce-scatter.5.cloned.1.call-update) | async-done | bytes 1048592 | tf_op jit(solution)/shard_map/reduce_scatter | solution.py:222
  781.5 4.8 fusion.123
  786.4 59.9 %reduce-scatter.9.cloned.1.call-done = f32[128,512]{1,0:T(8,128)} async-done(((f32[2048,512]{1,0:T(8,128)}), f32[128,512]{1,0:T(8,128)}) %reduce-scatter.9.cloned.1.call-update) | async-done | bytes 262160 | tf_op jit(solution)/shard_map/reduce_scatter | solution.py:310
  854.7 67.7 %reduce-scatter.11.cloned.1.call-done = f32[128,512]{1,0:T(8,128)} async-done(((f32[2048,512]{1,0:T(8,128)}), f32[128,512]{1,0:T(8,128)}) %reduce-scatter.11.cloned.1.call-update) | async-done | bytes 262160 | tf_op jit(solution)/shard_map/reduce_scatter | solution.py:311
  926.3 5.5 fusion.141
  937.5 6.7 fusion.66
  944.2 6.5 fusion.64
  950.8 6.9 fusion.60
  957.7 5.0 all-reduce.2
  967.2 64.4 %all-reduce = (f32[2048]{0:T(1024)}, f32[128]{0:T(128)}, f32[128]{0:T(128)}, f32[2048]{0:T(1024)}) all-reduce(f32[2048]{0:T(1024)S(1)} %get-tuple-element.661, bf16[128]{0:T(256)(128)(2,1)S(1)} %get-tuple-element.744, bf16[128]{0:T(256)(128)(2,1)S(1)} %get-tuple-element.745, ...), channel_id=1, replica_groups=mesh['tp'=2,'sp'=16] {'sp'}, use_global_device_ids=true, to_apply=%region_35.36 | all-reduce | flops 4352 | bytes 34304 | tf_op jit(solution)/shard_map/psum | solution.py:349
  1035.1 382.1 %all-reduce.13.cloned.1.call-done = (f32[1024,2048]{1,0:T(8,128)}, f32[512,2048]{1,0:T(8,128)}, f32[512,2048]{1,0:T(8,128)}, f32[8,2048]{1,0:T(8,128)}, f32[2048,1024]{1,0:T(8,128)}) async-done(((f32[1024,2048]{1,0:T(8,128)}, f32[512,2048]{1,0:T(8,128)}, f32[512,2048]{1,0:T(8,128)}, f32[8,2048]{1,0:T(8,128)}, f32[2048,1024]{1,0:T(8,128)}), (f32[1024,2048]{1,0:T(8,128)}, f32[512,2048]{1,0:T(8,128)}, ...) | async-done | bytes 25231376 | tf_op jit(solution)/shard_map/psum | solution.py:349
  1417.2 8.0 copy.216
  (328 shorter events, 152.2 us)
Async XLA Ops:
  7.2 49.6 %all-gather.7.cloned.1.call-start = ((), (), s32[]{:S(2)}) async-start(), calls=%async_computation.5 | async-start | bytes 2228224 | tf_op jit(solution)/shard_map/all_gather | solution.py:147
  8.6 15.9 %copy-start.48 = (f32[128]{0:T(128)}, f32[128]{0:T(128)S(1)}, u32[]{:S(2)}) copy-start(f32[128]{0:T(128)S(1)} %add_rsqrt_fusion.3) | copy-start | bytes 1540
  9.3 15.2 %copy-start.39 = (f32[2048]{0:T(1024)}, f32[2048]{0:T(1024)S(1)}, u32[]{:S(2)}) copy-start(f32[2048]{0:T(1024)S(1)} %convert_element_type.145) | copy-start | bytes 24580
  9.3 9.0 copy-start.1
  12.7 87.1 %all-gather.5.cloned.1.call-start = ((), (), s32[]{:S(2)}) async-start(), calls=%async_computation.4 | async-start | bytes 2228224 | tf_op jit(solution)/shard_map/all_gather | solution.py:146
  18.3 149.0 %all-reduce.9.cloned.1.call-start = ((), (), s32[]{:S(2)}) async-start(), calls=%async_computation.6 | async-start | bytes 1048576 | tf_op jit(solution)/shard_map/psum | solution.py:213
  24.8 570.5 %copy-start.43 = (f32[128,8]{0,1:T(8,128)}, f32[128,8]{0,1:T(8,128)S(1)}, u32[]{:S(2)}) copy-start(f32[128,8]{0,1:T(8,128)S(1)} %fusion.95) | copy-start | bytes 12292
  126.8 43.8 %copy-start.8 = (bf16[128,2048]{1,0:T(8,128)(2,1)S(1)}, bf16[128,2048]{1,0:T(8,128)(2,1)}, u32[]{:S(2)}) copy-start(bf16[128,2048]{1,0:T(8,128)(2,1)} %param.41) | copy-start | bytes 1572868
  131.4 168.4 %all-gather.11.cloned.1.call-start = ((), (), s32[]{:S(2)}) async-start(), calls=%async_computation.9 | async-start | bytes 17825792 | tf_op jit(solution)/shard_map/all_gather | solution.py:230
  168.6 421.2 %copy-start.54 = (f32[128]{0:T(128)}, f32[128]{0:T(128)S(1)}, u32[]{:S(2)}) copy-start(f32[128]{0:T(128)S(1)} %add_rsqrt_fusion.2) | copy-start | bytes 1540
  172.7 203.0 %all-gather.9.cloned.1.call-start = ((), (), s32[]{:S(2)}) async-start(), calls=%async_computation.7 | async-start | bytes 8912896 | tf_op jit(solution)/shard_map/all_gather | solution.py:219
  173.3 383.7 %reduce-scatter.7.cloned.1.call-start = ((), (), s32[]{:S(2)}) async-start(), calls=%async_computation.10 | async-start | bytes 17825792 | tf_op jit(solution)/shard_map/reduce_scatter | solution.py:243
  299.8 14.0 slice-start.2
  299.8 14.0 slice-start.3
  327.7 259.9 %all-reduce.11.cloned.1.call-start = ((), (), s32[]{:S(2)}) async-start(), calls=%async_computation.11 | async-start | bytes 1048576 | tf_op jit(solution)/shard_map/psum | solution.py:246
  559.2 211.2 %reduce-scatter.5.cloned.1.call-start = ((), (), s32[]{:S(2)}) async-start(), calls=%async_computation.8 | async-start | bytes 17825792 | tf_op jit(solution)/shard_map/reduce_scatter | solution.py:222
  574.5 13.2 copy-start.4
  574.5 271.8 %reduce-scatter.9.cloned.1.call-start = ((), (), s32[]{:S(2)}) async-start(), calls=%async_computation.12 | async-start | bytes 4456448 | tf_op jit(solution)/shard_map/reduce_scatter | solution.py:310
  589.8 9.3 copy-start.69
  589.8 9.3 copy-start.73
  635.5 286.9 %reduce-scatter.11.cloned.1.call-start = ((), (), s32[]{:S(2)}) async-start(), calls=%async_computation.13 | async-start | bytes 4456448 | tf_op jit(solution)/shard_map/reduce_scatter | solution.py:311
  640.3 134.9 %copy-start.44 = (f32[128,8]{0,1:T(8,128)S(1)}, f32[128,8]{0,1:T(8,128)}, u32[]{:S(2)}) copy-start(f32[128,8]{0,1:T(8,128)} %copy-done.43) | copy-start | bytes 12292
  640.3 135.2 %copy-start.28 = (f32[128,64]{1,0:T(8,128)S(1)}, f32[128,64]{1,0:T(8,128)}, u32[]{:S(2)}) copy-start(f32[128,64]{1,0:T(8,128)} %copy-done.27) | copy-start | bytes 98308
  640.3 135.2 %copy-start.35 = (f32[128,64]{1,0:T(8,128)S(1)}, f32[128,64]{1,0:T(8,128)}, u32[]{:S(2)}) copy-start(f32[128,64]{1,0:T(8,128)} %get-tuple-element.776) | copy-start | bytes 98308
  640.3 325.3 %all-reduce.15.cloned.1.call-start = ((), (), s32[]{:S(2)}) async-start(), calls=%async_computation.15 | async-start | bytes 2097152 | tf_op jit(solution)/shard_map/psum | solution.py:225
  781.5 67.8 %copy-start.18 = (f32[128,4,128]{2,1,0:T(4,128)S(1)}, f32[128,4,128]{2,1,0:T(4,128)}, u32[]{:S(2)}) copy-start(f32[128,4,128]{2,1,0:T(4,128)} %copy-done.17) | copy-start | bytes 786436
  854.7 71.6 %copy-start.21 = (bf16[128,1024]{1,0:T(8,128)(2,1)S(1)}, bf16[128,1024]{1,0:T(8,128)(2,1)}, u32[]{:S(2)}) copy-start(bf16[128,1024]{1,0:T(8,128)(2,1)} %copy-done.20) | copy-start | bytes 786436
  926.0 491.2 %all-reduce.13.cloned.1.call-start = ((), (), s32[]{:S(2)}) async-start(), calls=%async_computation.14 | async-start | bytes 50462720 | tf_op jit(solution)/shard_map/psum | solution.py:349
  950.7 14.9 %copy-start.51 = (f32[128]{0:T(128)S(1)}, f32[128]{0:T(128)}, u32[]{:S(2)}) copy-start(f32[128]{0:T(128)} %copy-done.48) | copy-start | bytes 1540
  950.7 16.5 %copy-start.45 = (f32[2048]{0:T(1024)S(1)}, f32[2048]{0:T(1024)}, u32[]{:S(2)}) copy-start(f32[2048]{0:T(1024)} %get-tuple-element.659) | copy-start | bytes 24580
  950.7 80.8 %copy-start.56 = (f32[128]{0:T(128)S(1)}, f32[128]{0:T(128)}, u32[]{:S(2)}) copy-start(f32[128]{0:T(128)} %copy-done.54) | copy-start | bytes 1540
  950.7 80.8 %copy-start.62 = (f32[128]{0:T(128)S(1)}, f32[128]{0:T(128)}, u32[]{:S(2)}) copy-start(f32[128]{0:T(128)} %copy-done.60) | copy-start | bytes 1540
  (63 other events, 275.1 us)
Sparse Core Ops, SparseCore 0:
  12.8 43.9 all-gather.6
  59.6 40.1 all-gather.4
  131.5 35.7 all-reduce.8
  172.9 126.8 all-gather.10
  302.6 73.0 all-gather.8
  380.2 176.7 reduce-scatter.6
  560.0 27.5 all-reduce.10
  591.8 178.5 reduce-scatter.4
  774.8 71.4 reduce-scatter.8
  851.0 71.3 reduce-scatter.10
  926.1 39.3 all-reduce.14
  972.2 444.9 all-reduce.12
